TPU v7x, 32 devices: a whole 2x2x4 slice. The times are simulated.
32 devices in a mesh: section: 2 (over core), expert: 4 (over y, x), tensor: 4 (over z).
Axes of the slice: x: 2, y: 2, z: 4, core: 2. Of those that a mesh axis runs over, the one named last changes fastest.
Arguments:
- inputs: float32 [1, 788, 768], P(None, 'expert'), may hold values from -6 to 6
- cotangent: float32 [1, 788, 768], P(None, 'expert'), may hold values from -6 to 6
- norm_scale: float32 [2, 2, 768], P('section'), may hold values from 0.5 to 1.5
- norm_shift: float32 [2, 2, 768], P('section'), may hold values from -3 to 3
- proj_weight: bfloat16 [2, 768, 3, 768], P('section', None, None, 'tensor'), may hold values from -0.21875 to 0.21875
- proj_bias: float32 [2, 2, 768], P('section', None, 'tensor'), may hold values from -3 to 3
- attn_weight: bfloat16 [2, 768, 768], P('section', 'tensor'), may hold values from -0.75 to 0.75
- attn_bias: float32 [2, 768], P('section'), may hold values from -3 to 3
- expert_in: bfloat16 [2, 4, 768, 3072], P('section', 'expert', None, 'tensor'), may hold values from -0.21875 to 0.21875
- expert_in_bias: float32 [2, 4, 3072], P('section', 'expert', 'tensor'), may hold values from -3 to 3
- expert_out: bfloat16 [2, 4, 3072, 768], P('section', 'expert', 'tensor'), may hold values from -0.109375 to 0.109375
- expert_out_bias: float32 [2, 4, 768], P('section', 'expert'), may hold values from -3 to 3
- routes: int32 [2, 1, 788, 2], P('section', None, 'expert'), may hold values from 0 to 3, all different within a row; in each aligned block of 197 rows (0 to 196, 197 to 393, ..., all dimensions but the last counted through in order) at most 148 rows name the same one
- gate_weights: float32 [2, 1, 788, 2], P('section', None, 'expert'), may hold values from 0.1 to 1
Outputs:
- section_out: float32 [2, 1, 788, 768], P('section', None, 'expert')
- section_in_grad: float32 [2, 1, 788, 768], P('section', None, 'expert')
- grad_norm_scale: float32 [2, 2, 768], P('section')
- grad_norm_shift: float32 [2, 2, 768], P('section')
- grad_proj_weight: float32 [2, 768, 3, 768], P('section', None, None, 'tensor')
- grad_proj_bias: float32 [2, 2, 768], P('section', None, 'tensor')
- grad_attn_weight: float32 [2, 768, 768], P('section', 'tensor')
- grad_attn_bias: float32 [2, 768], P('section')
- grad_expert_in: float32 [2, 4, 768, 3072], P('section', 'expert', None, 'tensor')
- grad_expert_in_bias: float32 [2, 4, 3072], P('section', 'expert', 'tensor')
- grad_expert_out: float32 [2, 4, 3072, 768], P('section', 'expert', 'tensor')
- grad_expert_out_bias: float32 [2, 4, 768], P('section', 'expert')
Inputs may be any that keep to these rules, and one draw needn't show every extreme that they name: `routes`: each row names 2 different experts. In the rows of one index of the expert axis for one section and micro-batch, no expert is named more than 148 times, and in every draw some expert is named exactly 148 times there.
All inputs are finite; a program needn't handle non-finite values.
Results may differ from a plain program's by a relative error of at most 0.015.
Values may be sent and summed in bfloat16 or wider, within the bound.
A program may use at most 128 MiB of HBM per device.

v0:
```python
import jax
import jax.numpy as jnp
from jax import lax
from jax.sharding import PartitionSpec as P

HEAD_DIM = 64
SEQ = 197
TOPK = 2


NORM_EPSILON = 1e-06
GELU_FACTOR = 0.7978845608028654
CUBIC_TERM = 0.044715


def from_behind(block, axis, distance):
    devices = range(lax.axis_size(axis))
    route = [(i - distance, i) for i in devices if i - distance in devices]
    return lax.ppermute(block, axis, route)


def gelu_value(pre_act):
    inner_arg = GELU_FACTOR * (pre_act + CUBIC_TERM * pre_act * pre_act * pre_act)
    return 0.5 * pre_act * (1.0 + jnp.tanh(inner_arg))


def gelu_slope(pre_act):
    tangent = jnp.tanh(GELU_FACTOR * (pre_act + CUBIC_TERM * pre_act * pre_act * pre_act))
    return 0.5 * (1.0 + tangent) + 0.5 * pre_act * (1.0 - tangent * tangent) * GELU_FACTOR * (
        1.0 + 3.0 * CUBIC_TERM * pre_act * pre_act
    )


def layer_norm(values, scale_row, shift_row):
    average = jnp.mean(values, axis=-1, keepdims=True)
    centred = values - average
    variance = jnp.mean(centred * centred, axis=-1, keepdims=True)
    inv_std = lax.rsqrt(variance + NORM_EPSILON)
    normed = centred * inv_std
    return (normed * scale_row + shift_row, normed, inv_std)


def norm_back(grad_normed, normed, inv_std, scale_row):
    scaled = grad_normed * scale_row
    return (
        scaled
        - jnp.mean(scaled, axis=-1, keepdims=True)
        - normed * jnp.mean(scaled * normed, axis=-1, keepdims=True)
    ) * inv_std


def slot_table(route_rows, experts, capacity):
    flat_ids = route_rows.reshape(-1)
    onehot = (flat_ids[:, None] == jnp.arange(experts, dtype=jnp.int32)[None, :]).astype(jnp.int32)
    before = jnp.cumsum(onehot, axis=0) - onehot
    position = jnp.sum(before * onehot, axis=1)
    return flat_ids * capacity + position


def slot_count(row_count, experts):
    return max(2, (3 * TOPK * row_count + 2 * experts - 1) // (2 * experts))


def attend(query_rows, key_rows, value_rows):
    scores = jnp.einsum(
        "ishe,ithe->ihst", query_rows, key_rows, preferred_element_type=jnp.float32
    ) * HEAD_DIM ** (-0.5)
    log_total = jnp.log(jnp.sum(jnp.exp(scores), axis=-1))
    prob_rows = jnp.exp(scores - log_total[..., None]).astype(jnp.bfloat16)
    attn_mixed = jnp.einsum(
        "ihst,ithe->ishe", prob_rows, value_rows, preferred_element_type=jnp.float32
    ).astype(jnp.bfloat16)
    return (attn_mixed, log_total)


def attend_back(query_rows, key_rows, value_rows, attn_mixed, log_total, grad_mixed):
    scale_factor = HEAD_DIM ** (-0.5)
    scores = (
        jnp.einsum("ishe,ithe->ihst", query_rows, key_rows, preferred_element_type=jnp.float32)
        * scale_factor
    )
    prob_f = jnp.exp(scores - log_total[..., None])
    prob_rows = prob_f.astype(jnp.bfloat16)
    grad_values = jnp.einsum(
        "ihst,ishe->ithe", prob_rows, grad_mixed, preferred_element_type=jnp.float32
    )
    grad_probs = jnp.einsum(
        "ishe,ithe->ihst", grad_mixed, value_rows, preferred_element_type=jnp.float32
    )
    row_delta = jnp.einsum(
        "ishe,ishe->ihs", grad_mixed, attn_mixed, preferred_element_type=jnp.float32
    )
    grad_scores = (prob_f * (grad_probs - row_delta[..., None]) * scale_factor).astype(jnp.bfloat16)
    grad_query = jnp.einsum(
        "ihst,ithe->ishe", grad_scores, key_rows, preferred_element_type=jnp.float32
    )
    grad_keys = jnp.einsum(
        "ihst,ishe->ithe", grad_scores, query_rows, preferred_element_type=jnp.float32
    )
    return (grad_query, grad_keys, grad_values)


def hand_over(values, by_step):
    return from_behind(values, "section", by_step)


def forward_block(inputs, weights, route_rows, gate_rows):
    (
        norm_scale,
        norm_shift,
        proj_weight,
        proj_bias,
        attn_weight,
        attn_bias,
        expert_in,
        expert_in_bias,
        expert_out,
        expert_out_bias,
    ) = weights
    row_count, model_width = inputs.shape
    images = row_count // SEQ
    local_width = proj_weight.shape[2]
    head_shape = (images, SEQ, local_width // HEAD_DIM, HEAD_DIM)
    normed_out, normed_first, inv_first = layer_norm(inputs, norm_scale[0], norm_shift[0])
    projected = jnp.einsum(
        "rd,dkf->rkf",
        normed_out.astype(jnp.bfloat16),
        proj_weight,
        preferred_element_type=jnp.float32,
    )
    query_rows = (projected[:, 0] + proj_bias[0]).astype(jnp.bfloat16).reshape(head_shape)
    key_rows = projected[:, 1].astype(jnp.bfloat16).reshape(head_shape)
    value_rows = (projected[:, 2] + proj_bias[1]).astype(jnp.bfloat16).reshape(head_shape)
    attn_mixed, log_total = attend(query_rows, key_rows, value_rows)
    partial_value = jnp.dot(
        attn_mixed.reshape(row_count, local_width), attn_weight, preferred_element_type=jnp.float32
    )
    hidden_res = inputs + (lax.psum(partial_value, "tensor") + attn_bias)
    normed_out_b, normed_second, inv_second = layer_norm(hidden_res, norm_scale[1], norm_shift[1])
    experts = lax.axis_size("expert")
    capacity = slot_count(row_count, experts)
    slot_ids = slot_table(route_rows, experts, capacity)
    repeated = jnp.repeat(normed_out_b.astype(jnp.bfloat16), TOPK, axis=0)
    outgoing = (
        jnp.zeros((experts * capacity, model_width), jnp.bfloat16)
        .at[slot_ids]
        .set(repeated)
        .reshape(experts, capacity, model_width)
    )
    quarter = model_width // lax.axis_size("tensor")
    col_start = lax.axis_index("tensor") * quarter
    bias_part = lax.dynamic_slice_in_dim(expert_out_bias, col_start, quarter, 0)
    incoming = lax.all_to_all(outgoing, "expert", split_axis=0, concat_axis=0, tiled=True)
    pre_act = (
        jnp.einsum("snd,dh->snh", incoming, expert_in, preferred_element_type=jnp.float32)
        + expert_in_bias
    )
    activated = gelu_value(pre_act).astype(jnp.bfloat16)
    partial_out = jnp.einsum(
        "snh,hd->snd", activated, expert_out, preferred_element_type=jnp.float32
    )
    summed = lax.psum_scatter(partial_out, "tensor", scatter_dimension=2, tiled=True)
    produced, pre_act, received = ((summed + bias_part).astype(jnp.bfloat16), pre_act, incoming)
    gate_column = gate_rows.reshape(-1, 1)
    full_rows = lax.all_gather(produced, "tensor", axis=2, tiled=True)
    returned = lax.all_to_all(full_rows, "expert", split_axis=0, concat_axis=0, tiled=True)
    picked = returned.reshape(experts * capacity, model_width)[slot_ids]
    branch = jnp.sum((gate_column * picked).reshape(row_count, TOPK, model_width), axis=1)
    block_out = hidden_res + branch
    kept_state = (
        normed_first,
        inv_first,
        query_rows,
        key_rows,
        value_rows,
        attn_mixed,
        log_total,
        normed_second,
        inv_second,
        slot_ids,
        gate_rows,
        received,
        pre_act,
    )
    return (block_out, kept_state)


def backward_block(cotangent, weights, kept_state):
    (
        norm_scale,
        norm_shift,
        proj_weight,
        proj_bias,
        attn_weight,
        attn_bias,
        expert_in,
        expert_in_bias,
        expert_out,
        expert_out_bias,
    ) = weights
    (
        normed_first,
        inv_first,
        query_rows,
        key_rows,
        value_rows,
        attn_mixed,
        log_total,
        normed_second,
        inv_second,
        slot_ids,
        gate_rows,
        received,
        pre_act,
    ) = kept_state
    row_count, model_width = cotangent.shape
    experts = lax.axis_size("expert")
    capacity = pre_act.shape[1]
    local_width = proj_weight.shape[2]
    quarter = model_width // lax.axis_size("tensor")
    grad_rows = (
        (gate_rows.reshape(row_count, TOPK, 1) * cotangent[:, None, :])
        .astype(jnp.bfloat16)
        .reshape(TOPK * row_count, model_width)
    )
    outgoing = (
        jnp.zeros((experts * capacity, model_width), jnp.bfloat16)
        .at[slot_ids]
        .set(grad_rows)
        .reshape(experts, capacity, model_width)
    )
    grad_out = lax.all_to_all(outgoing, "expert", split_axis=0, concat_axis=0, tiled=True)
    activated = gelu_value(pre_act).astype(jnp.bfloat16)
    grad_expert_out = jnp.einsum(
        "snh,snd->hd", activated, grad_out, preferred_element_type=jnp.float32
    )
    grad_expert_out_bias = jnp.sum(grad_out, axis=(0, 1), dtype=jnp.float32)
    grad_pre = jnp.einsum(
        "snd,hd->snh", grad_out, expert_out, preferred_element_type=jnp.float32
    ) * gelu_slope(pre_act)
    grad_expert_in_bias = jnp.sum(grad_pre, axis=(0, 1))
    grad_pre_b = grad_pre.astype(jnp.bfloat16)
    grad_expert_in = jnp.einsum(
        "snd,snh->dh", received, grad_pre_b, preferred_element_type=jnp.float32
    )
    partial_in = jnp.einsum(
        "snh,dh->snd", grad_pre_b, expert_in, preferred_element_type=jnp.float32
    )
    grad_buffer = lax.psum_scatter(partial_in, "tensor", scatter_dimension=2, tiled=True).astype(
        jnp.bfloat16
    )
    returned = lax.all_to_all(grad_buffer, "expert", split_axis=0, concat_axis=0, tiled=True)
    picked = returned.reshape(experts * capacity, quarter)[slot_ids]
    grad_cols = jnp.sum(picked.reshape(row_count, TOPK, quarter), axis=1, dtype=jnp.float32)
    grad_normed_b = lax.all_gather(grad_cols, "tensor", axis=1, tiled=True)
    grad_hidden = cotangent + norm_back(grad_normed_b, normed_second, inv_second, norm_scale[1])
    grad_hidden_b = grad_hidden.astype(jnp.bfloat16)
    grad_attn_bias = jnp.sum(grad_hidden, axis=0)
    mixed_flat = attn_mixed.reshape(row_count, local_width)
    grad_attn_weight = jnp.einsum(
        "rf,rd->fd", mixed_flat, grad_hidden_b, preferred_element_type=jnp.float32
    )
    grad_mixed = (
        jnp.einsum("rd,fd->rf", grad_hidden_b, attn_weight, preferred_element_type=jnp.float32)
        .astype(jnp.bfloat16)
        .reshape(attn_mixed.shape)
    )
    grad_query, grad_keys, grad_values = attend_back(
        query_rows, key_rows, value_rows, attn_mixed, log_total, grad_mixed
    )
    query_flat = grad_query.reshape(row_count, local_width)
    key_flat = grad_keys.reshape(row_count, local_width)
    value_flat = grad_values.reshape(row_count, local_width)
    grad_proj_bias = jnp.stack([jnp.sum(query_flat, axis=0), jnp.sum(value_flat, axis=0)])
    grad_proj = jnp.stack([query_flat, key_flat, value_flat], axis=1).astype(jnp.bfloat16)
    normed_a = (normed_first * norm_scale[0] + norm_shift[0]).astype(jnp.bfloat16)
    grad_proj_weight = jnp.einsum(
        "rd,rkf->dkf", normed_a, grad_proj, preferred_element_type=jnp.float32
    )
    partial_norm = jnp.einsum(
        "rkf,dkf->rd", grad_proj, proj_weight, preferred_element_type=jnp.float32
    )
    grad_normed_a = lax.psum(partial_norm, "tensor")
    grad_input = grad_hidden + norm_back(grad_normed_a, normed_first, inv_first, norm_scale[0])
    grad_norm_scale = jnp.stack(
        [
            jnp.sum(grad_normed_a * normed_first, axis=0),
            jnp.sum(grad_normed_b * normed_second, axis=0),
        ]
    )
    grad_norm_shift = jnp.stack([jnp.sum(grad_normed_a, axis=0), jnp.sum(grad_normed_b, axis=0)])
    mixer_part = (
        grad_norm_scale,
        grad_norm_shift,
        grad_proj_weight,
        grad_proj_bias,
        grad_attn_weight,
        grad_attn_bias,
    )
    expert_part = (grad_expert_in, grad_expert_in_bias, grad_expert_out, grad_expert_out_bias)
    return (grad_input, mixer_part, expert_part)


def on_device(
    inputs,
    cotangent,
    norm_scale,
    norm_shift,
    proj_weight,
    proj_bias,
    attn_weight,
    attn_bias,
    expert_in,
    expert_in_bias,
    expert_out,
    expert_out_bias,
    routes,
    gate_weights,
):
    weights = (
        norm_scale[0],
        norm_shift[0],
        proj_weight[0],
        proj_bias[0],
        attn_weight[0],
        attn_bias[0],
        expert_in[0, 0],
        expert_in_bias[0, 0],
        expert_out[0, 0],
        expert_out_bias[0, 0],
    )
    section_id = lax.axis_index("section")
    is_first = section_id == 0
    micro_count = inputs.shape[0]
    received = jnp.zeros_like(inputs[0])
    saved_keeps = []
    produced = []
    for tick_index in range(micro_count + 1):
        own_micro = jnp.clip(tick_index - section_id, 0, micro_count - 1)
        block_in = jnp.where(is_first, inputs[min(tick_index, micro_count - 1)], received)
        route_rows = lax.dynamic_index_in_dim(routes[0], own_micro, 0, keepdims=False)
        gate_rows = lax.dynamic_index_in_dim(gate_weights[0], own_micro, 0, keepdims=False)
        block_out, kept_state = forward_block(block_in, weights, route_rows, gate_rows)
        saved_keeps.append(kept_state)
        produced.append(block_out)
        if tick_index < micro_count:
            received = hand_over(block_out, 1)
    sent_back = jnp.zeros_like(inputs[0])
    mixer_sums = None
    expert_sums = None
    input_grads = []
    for tick_index in range(micro_count + 1):
        last_cotangent = cotangent[min(tick_index, micro_count - 1)]
        if tick_index == micro_count:
            last_cotangent = jnp.zeros_like(last_cotangent)
        block_grad = jnp.where(is_first, sent_back, last_cotangent)
        kept_state = jax.tree.map(
            lambda later_keep, early_keep: jnp.where(is_first, early_keep, later_keep),
            saved_keeps[min(tick_index + 1, micro_count)],
            saved_keeps[max(tick_index - 1, 0)],
        )
        grad_input, mixer_part, expert_part = backward_block(block_grad, weights, kept_state)
        mixer_sums = (
            mixer_part if mixer_sums is None else jax.tree.map(jnp.add, mixer_sums, mixer_part)
        )
        expert_sums = (
            expert_part if expert_sums is None else jax.tree.map(jnp.add, expert_sums, expert_part)
        )
        input_grads.append(grad_input)
        if tick_index < micro_count:
            sent_back = hand_over(grad_input, -1)
    section_out = jnp.stack([jnp.where(is_first, produced[0], produced[1])])
    section_in_grad = jnp.stack([jnp.where(is_first, input_grads[1], input_grads[0])])
    scale_sum, shift_sum, proj_sum, proj_bias_sum, attn_sum_w, attn_bias_sum = mixer_sums
    totals = lax.psum(
        (scale_sum, shift_sum, proj_sum, proj_bias_sum, attn_sum_w, attn_bias_sum), "expert"
    )
    grad_in_w, grad_in_b, grad_out_w, grad_out_b = expert_sums
    return (
        section_out[None],
        section_in_grad[None],
        totals[0][None],
        totals[1][None],
        totals[2][None],
        totals[3][None],
        totals[4][None],
        totals[5][None],
        grad_in_w[None, None],
        grad_in_b[None, None],
        grad_out_w[None, None],
        grad_out_b[None, None],
    )


def solution(mesh):
    in_specs = (
        P(None, "expert", None),
        P(None, "expert", None),
        P("section", None, None),
        P("section", None, None),
        P("section", None, None, "tensor"),
        P("section", None, "tensor"),
        P("section", "tensor", None),
        P("section", None),
        P("section", "expert", None, "tensor"),
        P("section", "expert", "tensor"),
        P("section", "expert", "tensor", None),
        P("section", "expert", None),
        P("section", None, "expert", None),
        P("section", None, "expert", None),
    )
    out_specs = (
        P("section", None, "expert", None),
        P("section", None, "expert", None),
        P("section", None, None),
        P("section", None, None),
        P("section", None, None, "tensor"),
        P("section", None, "tensor"),
        P("section", "tensor", None),
        P("section", None),
        P("section", "expert", None, "tensor"),
        P("section", "expert", "tensor"),
        P("section", "expert", "tensor", None),
        P("section", "expert", None),
    )
    return jax.shard_map(
        on_device, mesh=mesh, in_specs=in_specs, out_specs=out_specs, check_vma=False
    )
```

profile of v0, /device:TPU:0, one launch (start us, length us, event | category | flops | bytes accessed | tf_op | source)
XLA Modules:
  0.0 782.8 jit_solution(3827961485082313167)
XLA Ops:
  18.0 40.3 %all-reduce.9.cloned.1.call-done = f32[197,768]{1,0:T(8,128)} async-done(((f32[197,768]{1,0:T(8,128)}), f32[197,768]{1,0:T(8,128)}) %all-reduce.9.cloned.1.call-update) | async-done | bytes 605200 | tf_op jit(solution)/shard_map/psum | solution.py:138
  62.0 3.0 scatter_custom_fusion
  66.1 4.2 all-to-all-start
  70.5 12.0 %all-to-all-done = bf16[4,148,768]{2,1,0:T(8,128)(2,1)} async-done(((bf16[4,148,768]{2,1,0:T(8,128)(2,1)}), bf16[4,148,768]{2,1,0:T(8,128)(2,1)}, u32[]{:S(2)}, u32[]{:S(2)}) %all-to-all-start) | async-done | bytes 909344 | tf_op jit(solution)/shard_map/all_to_all | solution.py:153
  86.0 2.6 fusion.30
  88.5 4.3 copy.142
  92.8 4.5 reshape.717
  98.1 39.8 %reduce-scatter.13.cloned.1.call-done = f32[192,592]{1,0:T(8,128)} async-done(((f32[768,592]{1,0:T(8,128)}), f32[192,592]{1,0:T(8,128)}) %reduce-scatter.13.cloned.1.call-update) | async-done | bytes 454672
  142.2 29.4 %all_gather.12 = bf16[4,148,768]{1,0,2:T(4,128)(2,1)} all-gather(bf16[4,148,192]{1,0,2:T(4,128)(2,1)S(1)} %copy.93), channel_id=1, replica_groups=mesh['section'=2,'expert'=4,'tensor'=4] {'tensor'}, dimensions={2}, use_global_device_ids=true | all-gather | bytes 1136640 | tf_op jit(solution)/shard_map/all_gather | solution.py:165
  171.5 3.5 copy.94
  175.0 4.2 all-to-all-start.1
  180.3 9.9 %all-to-all-done.1 = bf16[4,148,768]{2,1,0:T(8,128)(2,1)} async-done(((bf16[4,148,768]{2,1,0:T(8,128)(2,1)}), bf16[4,148,768]{2,1,0:T(8,128)(2,1)}, u32[]{:S(2)}, u32[]{:S(2)}) %all-to-all-start.1) | async-done | bytes 909344 | tf_op jit(solution)/shard_map/all_to_all | solution.py:166
  191.6 2.7 gather_fusion
  194.3 2.8 reshape.627
  197.1 2.8 multiply_reduce_fusion.1
  207.2 40.7 %all-reduce.11.cloned.1.call-done = f32[197,768]{1,0:T(8,128)} async-done(((f32[197,768]{1,0:T(8,128)}), f32[197,768]{1,0:T(8,128)}) %all-reduce.11.cloned.1.call-update) | async-done | bytes 605200 | tf_op jit(solution)/shard_map/psum | solution.py:138
  252.2 3.0 scatter_custom_fusion.1
  256.4 4.8 all-to-all-start.2
  262.8 3.0 mul.457
  265.9 3.3 scatter_custom_fusion.2
  270.3 3.0 all-to-all-done.2
  273.2 3.5 all-to-all-start.4
  276.8 4.6 multiply_convert_fusion
  281.4 7.3 all-to-all-done.4
  288.7 5.2 fusion.129
  297.0 4.3 copy.146
  301.3 4.5 reshape.721
  306.5 4.4 fusion.28
  310.9 4.3 copy.144
  315.2 4.5 reshape.719
  319.8 26.7 %reduce-scatter.17.cloned.1.call-done = f32[192,592]{1,0:T(8,128)} async-done(((f32[768,592]{1,0:T(8,128)}), f32[192,592]{1,0:T(8,128)}) %reduce-scatter.17.cloned.1.call-update) | async-done | bytes 454672
  348.8 4.1 all-to-all-start.5
  352.9 37.0 %reduce-scatter.15.cloned.1.call-done = f32[192,592]{1,0:T(8,128)} async-done(((f32[768,592]{1,0:T(8,128)}), f32[192,592]{1,0:T(8,128)}) %reduce-scatter.15.cloned.1.call-update) | async-done | bytes 454672
  394.1 29.4 %all_gather.13 = bf16[4,148,768]{1,0,2:T(4,128)(2,1)} all-gather(bf16[4,148,192]{1,0,2:T(4,128)(2,1)S(1)} %copy.96), channel_id=1, replica_groups=mesh['section'=2,'expert'=4,'tensor'=4] {'tensor'}, dimensions={2}, use_global_device_ids=true | all-gather | bytes 1136640 | tf_op jit(solution)/shard_map/all_gather | solution.py:165
  423.5 3.5 copy.97
  427.0 4.3 all-to-all-start.3
  437.4 19.4 %all_gather.14 = f32[197,768]{0,1:T(8,128)S(1)} all-gather(f32[197,192]{0,1:T(8,128)S(1)} %copy.100), channel_id=1, replica_groups=mesh['section'=2,'expert'=4,'tensor'=4] {'tensor'}, dimensions={1}, use_global_device_ids=true | all-gather | bytes 756480 | tf_op jit(solution)/shard_map/all_gather | solution.py:255
  459.3 2.7 gather_fusion.1
  462.0 2.8 reshape.628
  464.8 2.9 multiply_reduce_fusion
  475.6 39.6 %all-reduce.13.cloned.1.call-done = f32[197,768]{1,0:T(8,128)} async-done(((f32[197,768]{1,0:T(8,128)}), f32[197,768]{1,0:T(8,128)}) %all-reduce.13.cloned.1.call-update) | async-done | bytes 605200 | tf_op jit(solution)/shard_map/psum | solution.py:283
  519.7 2.6 collective-permute-done.1
  524.6 3.0 mul.490
  527.6 4.0 scatter_custom_fusion.3
  531.6 2.3 reshape.622
  533.9 17.6 %all_to_all.40 = bf16[4,148,768]{2,1,0:T(8,128)(2,1)S(1)} all-to-all(bf16[4,148,768]{2,1,0:T(8,128)(2,1)} %reshape.622), channel_id=1, replica_groups=mesh['section'=2,'expert'=4,'tensor'=4] {'expert'}, dimensions={0} | all-to-all | bytes 1818624 | tf_op jit(solution)/shard_map/all_to_all | solution.py:232
  551.5 4.9 fusion.130
  559.6 4.3 copy.148
  563.8 4.5 reshape.723
  569.8 4.2 fusion.61
  575.8 32.2 %reduce-scatter.19.cloned.1.call-done = f32[192,592]{1,0:T(8,128)} async-done(((f32[768,592]{1,0:T(8,128)}), f32[192,592]{1,0:T(8,128)}) %reduce-scatter.19.cloned.1.call-update) | async-done | bytes 454672
  610.4 3.7 all-to-all-start.7
  614.0 2.6 fusion.103
  616.6 2.9 all-to-all-done.7
  619.6 2.6 gather_fusion.3
  628.1 18.3 %all_gather.15 = f32[197,768]{0,1:T(8,128)} all-gather(f32[197,192]{0,1:T(8,128)} %copy.107), channel_id=1, replica_groups=mesh['section'=2,'expert'=4,'tensor'=4] {'tensor'}, dimensions={1}, use_global_device_ids=true | all-gather | bytes 756480 | tf_op jit(solution)/shard_map/all_gather | solution.py:255
  658.9 4.1 fusion.131
  663.4 2.6 copy.115
  667.4 4.4 fusion
  671.8 3.9 fusion.1
  676.0 18.1 %all-reduce.15.cloned.1.call-done = f32[197,768]{1,0:T(8,128)} async-done(((f32[197,768]{1,0:T(8,128)}), f32[197,768]{1,0:T(8,128)}) %all-reduce.15.cloned.1.call-update) | async-done | bytes 605200 | tf_op jit(solution)/shard_map/psum | solution.py:283
  698.4 17.9 %all-reduce.1 = (f32[1,2,768]{2,1,0:T(2,128)}, f32[1,2,768]{2,1,0:T(2,128)}, f32[1,2,192]{2,1,0:T(2,128)}, f32[1,768]{1,0:T(1,128)}) all-reduce(f32[1,2,768]{2,1,0:T(2,128)S(1)} %fusion.106, f32[1,2,768]{2,1,0:T(2,128)S(1)} %fusion.107, f32[1,2,192]{2,1,0:T(2,128)S(1)} %fusion.108, ...), channel_id=1, replica_groups=mesh['section'=2,'expert'=4,'tensor'=4] {'expert'}, use_global_device_ids=true, to_apply=%region_41.42 | all-reduce | flops 4224 | bytes 33792 | tf_op jit(solution)/shard_map/psum | solution.py:375
  716.3 55.8 %all-reduce.17.cloned.1.call-done = (f32[1,768,3,192]{1,3,2,0:T(8,128)}, f32[1,192,768]{2,1,0:T(8,128)}) async-done(((f32[1,768,3,192]{1,3,2,0:T(8,128)}, f32[1,192,768]{2,1,0:T(8,128)}), (f32[1,768,3,192]{1,3,2,0:T(8,128)}, f32[1,192,768]{2,1,0:T(8,128)})) %all-reduce.17.cloned.1.call-update) | async-done | bytes 2359312 | tf_op jit(solution)/shard_map/psum | solution.py:375
  772.1 2.9 copy.183
  (418 shorter events, 108.5 us)
Async XLA Ops:
  7.2 75.3 %copy-start = (bf16[1,1,768,768]{3,2,1,0:T(8,128)(2,1)S(1)}, bf16[1,1,768,768]{3,2,1,0:T(8,128)(2,1)}, u32[]{:S(2)}) copy-start(bf16[1,1,768,768]{3,2,1,0:T(8,128)(2,1)} %param.22) | copy-start | bytes 3538948
  7.2 51.1 %all-reduce.9.cloned.1.call-start = ((), (), s32[]{:S(2)}) async-start(), calls=%async_computation.12 | async-start | bytes 1228800 | tf_op jit(solution)/shard_map/psum | solution.py:138
  8.5 4.9 copy-start.78
  8.5 4.9 copy-start.106
  13.6 191.1 %copy-start.65 = (f32[3,64]{1,0:T(4,128)}, f32[3,64]{1,0:T(4,128)S(1)}, u32[]{:S(2)}) copy-start(f32[3,64]{1,0:T(4,128)S(1)} %add.382) | copy-start | bytes 2308
  14.0 44.3 %copy-start.2 = (f32[1,197,768]{2,0,1:T(1,128)S(1)}, f32[1,197,768]{2,0,1:T(1,128)}, u32[]{:S(2)}) copy-start(f32[1,197,768]{2,0,1:T(1,128)} %param.14) | copy-start | bytes 1815556
  14.2 45.3 %copy-start.32 = (bf16[197,3,64]{0,2,1:T(8,128)(2,1)}, bf16[197,3,64]{0,2,1:T(8,128)(2,1)S(1)}, u32[]{:S(2)}) copy-start(bf16[197,3,64]{0,2,1:T(8,128)(2,1)S(1)} %add_convert_fusion.11) | copy-start | bytes 226948
  14.4 45.1 %copy-start.54 = (bf16[3,64,197]{2,1,0:T(8,128)(2,1)}, bf16[3,64,197]{2,1,0:T(8,128)(2,1)S(1)}, u32[]{:S(2)}) copy-start(bf16[3,64,197]{2,1,0:T(8,128)(2,1)S(1)} %convolution_convert_fusion.5) | copy-start | bytes 226948
  18.0 44.1 %copy-start.95 = (s32[394,1]{0,1:T(1,128)}, s32[394,1]{0,1:T(1,128)S(1)}, u32[]{:S(2)}) copy-start(s32[394,1]{0,1:T(1,128)S(1)} %compare_select_fusion) | copy-start | bytes 4732
  59.5 5.5 copy-start.71
  59.8 5.3 copy-start.87
  59.8 5.2 copy-start.79
  65.0 5.4 copy-start.105
  66.1 16.4 %all-to-all-start = ((bf16[4,148,768]{2,1,0:T(8,128)(2,1)}), bf16[4,148,768]{2,1,0:T(8,128)(2,1)}, u32[]{:S(2)}, u32[]{:S(2)}) async-start(bf16[4,148,768]{2,1,0:T(8,128)(2,1)} %reshape.612), calls=%async_computation | async-start | bytes 1867776 | tf_op jit(solution)/shard_map/all_to_all | solution.py:153
  70.4 67.6 %reduce-scatter.13.cloned.1.call-start = ((), (), s32[]{:S(2)}) async-start(), calls=%async_computation.16 | async-start | bytes 2457600
  70.5 14.2 %copy-start.101 = (f32[768]{0:T(1024)}, f32[768]{0:T(1024)S(1)}, u32[]{:S(2)}) copy-start(f32[768]{0:T(1024)S(1)} %reduce.18) | copy-start | bytes 9220
  98.1 44.0 %copy-start.89 = (f32[1,1,192]{2,1,0:T(1,128)}, f32[1,1,192]{2,1,0:T(1,128)S(1)}, u32[]{:S(2)}) copy-start(f32[1,1,192]{2,1,0:T(1,128)S(1)} %constant_dynamic-slice_fusion) | copy-start | bytes 2308
  171.5 8.0 %copy-start.93 = (f32[1,1,197,2]{2,3,1,0:T(2,128)S(1)}, f32[1,1,197,2]{2,3,1,0:T(2,128)}, u32[]{:S(2)}) copy-start(f32[1,1,197,2]{2,3,1,0:T(2,128)} %param.27) | copy-start | bytes 4732
  171.5 8.8 %copy-start.96 = (s32[394,1]{0,1:T(1,128)S(1)}, s32[394,1]{0,1:T(1,128)}, u32[]{:S(2)}) copy-start(s32[394,1]{0,1:T(1,128)} %copy-done.95) | copy-start | bytes 4732
  175.0 15.2 %all-to-all-start.1 = ((bf16[4,148,768]{2,1,0:T(8,128)(2,1)}), bf16[4,148,768]{2,1,0:T(8,128)(2,1)}, u32[]{:S(2)}, u32[]{:S(2)}) async-start(bf16[4,148,768]{2,1,0:T(8,128)(2,1)} %copy.94), calls=%async_computation.1 | async-start | bytes 1867776 | tf_op jit(solution)/shard_map/all_to_all | solution.py:166
  179.3 68.6 %all-reduce.11.cloned.1.call-start = ((), (), s32[]{:S(2)}) async-start(), calls=%async_computation.13 | async-start | bytes 1228800 | tf_op jit(solution)/shard_map/psum | solution.py:138
  200.0 3.1 collective-permute-start
  205.8 43.3 %copy-start.34 = (bf16[197,3,64]{0,2,1:T(8,128)(2,1)}, bf16[197,3,64]{0,2,1:T(8,128)(2,1)S(1)}, u32[]{:S(2)}) copy-start(bf16[197,3,64]{0,2,1:T(8,128)(2,1)S(1)} %add_convert_fusion.9) | copy-start | bytes 226948
  206.0 43.4 %copy-start.56 = (bf16[3,64,197]{2,1,0:T(8,128)(2,1)}, bf16[3,64,197]{2,1,0:T(8,128)(2,1)S(1)}, u32[]{:S(2)}) copy-start(bf16[3,64,197]{2,1,0:T(8,128)(2,1)S(1)} %convolution_convert_fusion.4) | copy-start | bytes 226948
  206.1 43.3 %copy-start.88 = (f32[197]{0:T(256)S(1)}, f32[197]{0:T(256)}, u32[]{:S(2)}) copy-start(f32[197]{0:T(256)} %copy-done.87) | copy-start | bytes 2368
  249.2 6.1 copy-start.73
  250.0 5.2 copy-start.83
  255.2 5.9 copy-start.94
  256.4 4.9 copy-start.27
  256.4 16.9 %all-to-all-start.2 = ((bf16[4,148,768]{2,1,0:T(8,128)(2,1)}), bf16[4,148,768]{2,1,0:T(8,128)(2,1)}, u32[]{:S(2)}, u32[]{:S(2)}) async-start(bf16[4,148,768]{2,1,0:T(8,128)(2,1)} %reshape.616), calls=%async_computation.2 | async-start | bytes 1867776 | tf_op jit(solution)/shard_map/all_to_all | solution.py:153
  273.2 15.4 %all-to-all-start.4 = ((bf16[4,148,768]{2,1,0:T(8,128)(2,1)}), bf16[4,148,768]{2,1,0:T(8,128)(2,1)S(1)}, u32[]{:S(2)}, u32[]{:S(2)}) async-start(bf16[4,148,768]{2,1,0:T(8,128)(2,1)} %reshape.618), calls=%async_computation.4 | async-start | bytes 1867776 | tf_op jit(solution)/shard_map/all_to_all | solution.py:232
  276.8 69.7 %reduce-scatter.17.cloned.1.call-start = ((), (), s32[]{:S(2)}) async-start(), calls=%async_computation.18 | async-start | bytes 2457600
  288.7 5.2 copy-start.19
  305.9 84.1 %reduce-scatter.15.cloned.1.call-start = ((), (), s32[]{:S(2)}) async-start(), calls=%async_computation.17 | async-start | bytes 2457600
  347.8 44.9 %copy-start.90 = (f32[1,1,192]{2,1,0:T(1,128)S(1)}, f32[1,1,192]{2,1,0:T(1,128)}, u32[]{:S(2)}) copy-start(f32[1,1,192]{2,1,0:T(1,128)} %copy-done.89) | copy-start | bytes 2308
  348.8 78.2 %all-to-all-start.5 = ((bf16[4,148,192]{2,1,0:T(8,128)(2,1)}), bf16[4,148,192]{2,1,0:T(8,128)(2,1)}, u32[]{:S(2)}, u32[]{:S(2)}) async-start(bf16[4,148,192]{2,1,0:T(8,128)(2,1)} %copy.147), calls=%async_computation.5 | async-start | bytes 622592 | tf_op jit(solution)/shard_map/all_to_all | solution.py:252
  423.5 8.0 %copy-start.31 = (f32[197,1,192]{0,2,1:T(8,128)S(1)}, f32[197,1,192]{0,2,1:T(8,128)}, u32[]{:S(2)}) copy-start(f32[197,1,192]{0,2,1:T(8,128)} %copy-done.30) | copy-start | bytes 453892
  423.5 8.0 %copy-start.51 = (bf16[197,1,192]{0,2,1:T(8,128)(2,1)S(1)}, bf16[197,1,192]{0,2,1:T(8,128)(2,1)}, u32[]{:S(2)}) copy-start(bf16[197,1,192]{0,2,1:T(8,128)(2,1)} %copy-done.50) | copy-start | bytes 226948
  423.5 8.0 %copy-start.53 = (bf16[197,1,192]{0,2,1:T(8,128)(2,1)S(1)}, bf16[197,1,192]{0,2,1:T(8,128)(2,1)}, u32[]{:S(2)}) copy-start(bf16[197,1,192]{0,2,1:T(8,128)(2,1)} %copy-done.52) | copy-start | bytes 226948
  423.5 8.0 %copy-start.66 = (f32[3,64]{1,0:T(4,128)S(1)}, f32[3,64]{1,0:T(4,128)}, u32[]{:S(2)}) copy-start(f32[3,64]{1,0:T(4,128)} %copy-done.65) | copy-start | bytes 2308
  427.0 5.2 copy-start.75
  427.0 30.9 %all-to-all-start.3 = ((bf16[4,148,768]{2,1,0:T(8,128)(2,1)}), bf16[4,148,768]{2,1,0:T(8,128)(2,1)}, u32[]{:S(2)}, u32[]{:S(2)}) async-start(bf16[4,148,768]{2,1,0:T(8,128)(2,1)} %copy.97), calls=%async_computation.3 | async-start | bytes 1867776 | tf_op jit(solution)/shard_map/all_to_all | solution.py:166
  431.4 83.9 %all-reduce.13.cloned.1.call-start = ((), (), s32[]{:S(2)}) async-start(), calls=%async_computation.14 | async-start | bytes 1228800 | tf_op jit(solution)/shard_map/psum | solution.py:283
  461.9 5.8 copy-start.4
  461.9 5.8 copy-start.72
  461.9 5.8 copy-start.74
  461.9 5.8 copy-start.80
  462.0 5.8 copy-start.84
  472.7 42.6 %copy-start.70 = (f32[197]{0:T(256)S(1)}, f32[197]{0:T(256)}, u32[]{:S(2)}) copy-start(f32[197]{0:T(256)} %copy-done.69) | copy-start | bytes 2368
  472.7 42.6 %copy-start.77 = (f32[197]{0:T(256)S(1)}, f32[197]{0:T(256)}, u32[]{:S(2)}) copy-start(f32[197]{0:T(256)} %copy-done.76) | copy-start | bytes 2368
  475.6 132.5 %reduce-scatter.19.cloned.1.call-start = ((), (), s32[]{:S(2)}) async-start(), calls=%async_computation.19 | async-start | bytes 2457600
  518.4 9.2 %copy-start.25 = (f32[197,768]{1,0:T(8,128)}, f32[197,768]{1,0:T(8,128)S(1)}, u32[]{:S(2)}) copy-start(f32[197,768]{1,0:T(8,128)S(1)} %multiply_add_fusion.4) | copy-start | bytes 1815556
  518.4 3.9 collective-permute-start.1
  531.6 19.9 %copy-start.103 = (f32[768]{0:T(1024)S(1)}, f32[768]{0:T(1024)}, u32[]{:S(2)}) copy-start(f32[768]{0:T(1024)} %copy-done.101) | copy-start | bytes 9220
  533.9 17.7 %copy-start.108 = (bf16[1,1,768,768]{3,2,1,0:T(8,128)(2,1)S(1)}, bf16[1,1,768,768]{3,2,1,0:T(8,128)(2,1)}, u32[]{:S(2)}) copy-start(bf16[1,1,768,768]{3,2,1,0:T(8,128)(2,1)} %param.24) | copy-start | bytes 3538948
  551.5 4.9 copy-start.20
  569.8 5.0 copy-start.6
  569.8 5.0 copy-start.42
  610.4 9.2 %all-to-all-start.7 = ((bf16[4,148,192]{2,1,0:T(8,128)(2,1)}), bf16[4,148,192]{2,1,0:T(8,128)(2,1)S(1)}, u32[]{:S(2)}, u32[]{:S(2)}) async-start(bf16[4,148,192]{2,1,0:T(8,128)(2,1)} %copy.149), calls=%async_computation.7 | async-start | bytes 622592 | tf_op jit(solution)/shard_map/all_to_all | solution.py:252
  614.0 80.1 %all-reduce.15.cloned.1.call-start = ((), (), s32[]{:S(2)}) async-start(), calls=%async_computation.15 | async-start | bytes 1228800 | tf_op jit(solution)/shard_map/psum | solution.py:283
  622.2 26.4 %copy-start.8 = (f32[197,768]{1,0:T(8,128)S(1)}, f32[197,768]{1,0:T(8,128)}, u32[]{:S(2)}) copy-start(f32[197,768]{1,0:T(8,128)} %copy-done.7) | copy-start | bytes 1815556
  655.6 116.5 %all-reduce.17.cloned.1.call-start = ((), (), s32[]{:S(2)}) async-start(), calls=%async_computation.20 | async-start | bytes 4718592 | tf_op jit(solution)/shard_map/psum | solution.py:375
  658.9 4.5 copy-start.92
  675.7 19.9 %copy-start.81 = (f32[197]{0:T(256)S(1)}, f32[197]{0:T(256)}, u32[]{:S(2)}) copy-start(f32[197]{0:T(256)} %get-tuple-element.115) | copy-start | bytes 2368
  (69 other events, 160.8 us)
Sparse Core Ops, SparseCore 0:
  15.7 42.5 all-reduce.8
  97.5 40.4 reduce-scatter.12
  207.3 40.5 all-reduce.10
  306.0 40.4 reduce-scatter.16
  349.2 40.6 reduce-scatter.14
  475.7 39.5 all-reduce.12
  568.5 39.4 reduce-scatter.18
  655.7 38.4 all-reduce.14
  697.9 74.1 all-reduce.16
where the time goes:
time: 794 us; the launch traced here: 783 us
  waiting for transfers between devices  370 us (47%)
  blocking collectives  132 us (17%)
  local copies, waits for them, and re-layouts  126 us (16%)
  matrix products  63.3 us (8%)
  other arithmetic  43 us (5%)
  starting transfers between devices  32.6 us (4%)
  between operations  16.1 us (2%)
    unnamed x13, waiting for transfers between devices  136 us
    psum x2, waiting for transfers between devices, forward_block(): hidden_res = inputs + (lax.psum(partial_value, 'tensor') + attn_bias)  81 us
    unnamed x253, local copies, waits for them, and re-layouts  61.4 us
    all_gather x2, blocking collectives, forward_block(): full_rows = lax.all_gather(produced, 'tensor', axis=2, tiled=True)  58.7 us
    psum x2, waiting for transfers between devices, backward_block(): grad_normed_a = lax.psum(partial_norm, 'tensor')  57.8 us
    psum x1, waiting for transfers between devices, on_device(): lax.psum((scale_sum, shift_sum, proj_sum, proj_bias_sum, attn_sum_w, attn...  55.8 us
    all_gather x2, blocking collectives, backward_block(): grad_normed_b = lax.all_gather(grad_cols, 'tensor', axis=1, tiled=True)  37.7 us
    psum x1, blocking collectives, on_device(): lax.psum((scale_sum, shift_sum, proj_sum, proj_bias_sum, attn_sum_w, attn...  17.9 us
  transfers between devices with their start and end apart: 18, of which 16 were waited for; matrix products, arithmetic and copies ran while one was open for 10% of the time, Pallas kernels for 0%

commit v1 on v0

v1 whole, which is shorter than its diff:
```python
import functools
import itertools

import jax
import jax.numpy as jnp
from jax import lax
from jax.experimental import pallas as pl
from jax.experimental.pallas import tpu as pltpu
from jax.sharding import PartitionSpec as P

HEAD_DIM = 64
SEQ = 197
TOPK = 2


NORM_EPSILON = 1e-06
GELU_FACTOR = 0.7978845608028654
CUBIC_TERM = 0.044715


MESH = pl.DeviceIdType.MESH
ROW_TILE = 16
BF16 = jnp.bfloat16
F32 = jnp.float32


def from_behind(block, axis, distance):
    devices = range(lax.axis_size(axis))
    route = [(i - distance, i) for i in devices if i - distance in devices]
    return lax.ppermute(block, axis, route)


def flat_index(places, sizes):
    total = places[0]
    for place, size in zip(places[1:], sizes[1:]):
        total = total * size + place
    return total


def partners(axes, sizes):
    here = [lax.axis_index(axis) for axis in axes]
    others = []
    for offsets in itertools.product(*[range(size) for size in sizes]):
        if any(offsets):
            there = [
                lax.rem(place + offset, size) if offset else place
                for place, offset, size in zip(here, offsets, sizes)
            ]
            others.append((flat_index(there, sizes), dict(zip(axes, there))))
    return flat_index(here, sizes), others


def greet(others):
    barrier = pltpu.get_barrier_semaphore()
    for _, device in others:
        pl.semaphore_signal(barrier, inc=1, device_id=device, device_id_type=MESH)
    pl.semaphore_wait(barrier, len(others))


def when_active(active, body):
    if active is None:
        body()
    else:
        pl.when(lax.axis_index("section") == active)(body)


def send(source, target, send_sem, recv_sem, device):
    copy = pltpu.make_async_remote_copy(
        src_ref=source,
        dst_ref=target,
        send_sem=send_sem,
        recv_sem=recv_sem,
        device_id=device,
        device_id_type=MESH,
    )
    copy.start()
    return copy


def exchange_kernel(axes, sizes, active, gather, x_ref, o_ref, send_sem, recv_sem):
    def body():
        me, others = partners(axes, sizes)
        greet(others)
        copies = [
            send(
                x_ref if gather else x_ref.at[index],
                o_ref.at[me],
                send_sem.at[k],
                recv_sem.at[k],
                device,
            )
            for k, (index, device) in enumerate(others)
        ]
        o_ref[me] = x_ref[...] if gather else x_ref[me]
        for copy in copies:
            copy.wait()

    when_active(active, body)


def reduce_kernel(axes, sizes, active, count, *refs):
    parts, sums, landed = refs[:count], refs[count : 2 * count], refs[2 * count : 3 * count]
    send_sem, recv_sem = refs[3 * count :]

    def body():
        me, others = partners(axes, sizes)
        greet(others)
        first = [
            [
                send(
                    parts[a].at[index],
                    landed[a].at[k],
                    send_sem.at[0, a, k],
                    recv_sem.at[0, a, k],
                    device,
                )
                for k, (index, device) in enumerate(others)
            ]
            for a in range(count)
        ]
        second = []
        for a in range(count):
            for copy in first[a]:
                copy.wait()
            total = parts[a][me].astype(F32)
            for k in range(len(others)):
                total = total + landed[a][k].astype(F32)
            sums[a][me] = total.astype(sums[a].dtype)
            for k, (_, device) in enumerate(others):
                second.append(
                    send(
                        sums[a].at[me],
                        sums[a].at[me],
                        send_sem.at[1, a, k],
                        recv_sem.at[1, a, k],
                        device,
                    )
                )
        for copy in second:
            copy.wait()

    when_active(active, body)


class Links:
    def __init__(self):
        self.ids = itertools.count()

    def call(self, kernel, name, out_shape, scratch_shapes, operands):
        in_vmem = pl.BlockSpec(memory_space=pltpu.VMEM)
        return pl.pallas_call(
            kernel,
            out_shape=out_shape,
            in_specs=[in_vmem] * len(operands),
            out_specs=[in_vmem] * len(out_shape),
            scratch_shapes=scratch_shapes,
            compiler_params=pltpu.CompilerParams(
                collective_id=next(self.ids), has_side_effects=True
            ),
            name=name,
        )(*operands)

    def exchange(self, blocks, axes, active, gather=False):
        sizes = [lax.axis_size(axis) for axis in axes]
        members = 1
        for size in sizes:
            members *= size
        shape = (members,) + blocks.shape if gather else blocks.shape
        sems = pltpu.SemaphoreType.DMA((members - 1,))
        return self.call(
            functools.partial(exchange_kernel, axes, sizes, active, gather),
            "gather" if gather else "exchange",
            [jax.ShapeDtypeStruct(shape, blocks.dtype)],
            [sems, sems],
            [blocks],
        )[0]

    def all_sum(self, arrays, axes, active):
        sizes = [lax.axis_size(axis) for axis in axes]
        members = arrays[0].shape[0]
        sems = pltpu.SemaphoreType.DMA((2, len(arrays), members - 1))
        return self.call(
            functools.partial(reduce_kernel, axes, sizes, active, len(arrays)),
            "all_sum",
            [jax.ShapeDtypeStruct(a.shape, a.dtype) for a in arrays],
            [pltpu.VMEM((members - 1,) + a.shape[1:], a.dtype) for a in arrays] + [sems, sems],
            arrays,
        )

    def sum_rows(self, partial_rows, axis, active):
        rows, width = partial_rows.shape
        members = lax.axis_size(axis)
        chunk = -(-rows // (members * ROW_TILE)) * ROW_TILE
        padded = jnp.pad(partial_rows.astype(BF16), ((0, members * chunk - rows), (0, 0)))
        total = self.all_sum([padded.reshape(members, chunk, width)], (axis,), active)[0]
        return total.reshape(members * chunk, width)[:rows].astype(F32)

    def join_columns(self, columns, active):
        rows, width = columns.shape
        pieces = self.exchange(columns.astype(BF16), ("tensor",), active, gather=True)
        return jnp.concatenate([pieces[k] for k in range(pieces.shape[0])], axis=1).astype(F32)


def gelu_value(pre_act):
    inner_arg = GELU_FACTOR * (pre_act + CUBIC_TERM * pre_act * pre_act * pre_act)
    return 0.5 * pre_act * (1.0 + jnp.tanh(inner_arg))


def gelu_slope(pre_act):
    tangent = jnp.tanh(GELU_FACTOR * (pre_act + CUBIC_TERM * pre_act * pre_act * pre_act))
    return 0.5 * (1.0 + tangent) + 0.5 * pre_act * (1.0 - tangent * tangent) * GELU_FACTOR * (
        1.0 + 3.0 * CUBIC_TERM * pre_act * pre_act
    )


def layer_norm(values, scale_row, shift_row):
    average = jnp.mean(values, axis=-1, keepdims=True)
    centred = values - average
    variance = jnp.mean(centred * centred, axis=-1, keepdims=True)
    inv_std = lax.rsqrt(variance + NORM_EPSILON)
    normed = centred * inv_std
    return (normed * scale_row + shift_row, normed, inv_std)


def norm_back(grad_normed, normed, inv_std, scale_row):
    scaled = grad_normed * scale_row
    return (
        scaled
        - jnp.mean(scaled, axis=-1, keepdims=True)
        - normed * jnp.mean(scaled * normed, axis=-1, keepdims=True)
    ) * inv_std


def slot_table(route_rows, experts, capacity):
    flat_ids = route_rows.reshape(-1)
    onehot = (flat_ids[:, None] == jnp.arange(experts, dtype=jnp.int32)[None, :]).astype(jnp.int32)
    before = jnp.cumsum(onehot, axis=0) - onehot
    position = jnp.sum(before * onehot, axis=1)
    return flat_ids * capacity + position


def slot_count(row_count, experts):
    return max(2, (3 * TOPK * row_count + 2 * experts - 1) // (2 * experts))


def attend(query_rows, key_rows, value_rows):
    scores = jnp.einsum(
        "ishe,ithe->ihst", query_rows, key_rows, preferred_element_type=jnp.float32
    ) * HEAD_DIM ** (-0.5)
    log_total = jnp.log(jnp.sum(jnp.exp(scores), axis=-1))
    prob_rows = jnp.exp(scores - log_total[..., None]).astype(jnp.bfloat16)
    attn_mixed = jnp.einsum(
        "ihst,ithe->ishe", prob_rows, value_rows, preferred_element_type=jnp.float32
    ).astype(jnp.bfloat16)
    return (attn_mixed, log_total)


def attend_back(query_rows, key_rows, value_rows, attn_mixed, log_total, grad_mixed):
    scale_factor = HEAD_DIM ** (-0.5)
    scores = (
        jnp.einsum("ishe,ithe->ihst", query_rows, key_rows, preferred_element_type=jnp.float32)
        * scale_factor
    )
    prob_f = jnp.exp(scores - log_total[..., None])
    prob_rows = prob_f.astype(jnp.bfloat16)
    grad_values = jnp.einsum(
        "ihst,ishe->ithe", prob_rows, grad_mixed, preferred_element_type=jnp.float32
    )
    grad_probs = jnp.einsum(
        "ishe,ithe->ihst", grad_mixed, value_rows, preferred_element_type=jnp.float32
    )
    row_delta = jnp.einsum(
        "ishe,ishe->ihs", grad_mixed, attn_mixed, preferred_element_type=jnp.float32
    )
    grad_scores = (prob_f * (grad_probs - row_delta[..., None]) * scale_factor).astype(jnp.bfloat16)
    grad_query = jnp.einsum(
        "ihst,ithe->ishe", grad_scores, key_rows, preferred_element_type=jnp.float32
    )
    grad_keys = jnp.einsum(
        "ihst,ishe->ithe", grad_scores, query_rows, preferred_element_type=jnp.float32
    )
    return (grad_query, grad_keys, grad_values)


def column_parts(rows, weight, experts, transposed):
    members = lax.axis_size("tensor")
    count = rows.shape[0]
    if transposed:
        width = weight.shape[0] // members
        parts = [
            lax.dot_general(
                rows,
                weight[k * width : (k + 1) * width],
                (((1,), (1,)), ((), ())),
                preferred_element_type=F32,
            )
            for k in range(members)
        ]
    else:
        width = weight.shape[1] // members
        parts = [
            jnp.dot(rows, weight[:, k * width : (k + 1) * width], preferred_element_type=F32)
            for k in range(members)
        ]
    return parts, (members * experts, count // experts, width)


def forward_block(links, active, inputs, weights, picks, gate_rows):
    (
        norm_scale,
        norm_shift,
        proj_weight,
        proj_bias,
        attn_weight,
        attn_bias,
        expert_in,
        expert_in_bias,
        expert_out,
        expert_out_bias,
    ) = weights
    row_count, model_width = inputs.shape
    images = row_count // SEQ
    local_width = proj_weight.shape[2]
    head_shape = (images, SEQ, local_width // HEAD_DIM, HEAD_DIM)
    experts = lax.axis_size("expert")
    members = lax.axis_size("tensor")
    slots = picks.shape[2]
    capacity = slots // experts
    normed_out, normed_first, inv_first = layer_norm(inputs, norm_scale[0], norm_shift[0])
    normed_a = normed_out.astype(BF16)
    query_rows, key_rows, value_rows = [
        jnp.dot(normed_a, proj_weight[:, k], preferred_element_type=F32) for k in range(3)
    ]
    query_rows = (query_rows + proj_bias[0]).astype(BF16).reshape(head_shape)
    key_rows = key_rows.astype(BF16).reshape(head_shape)
    value_rows = (value_rows + proj_bias[1]).astype(BF16).reshape(head_shape)
    attn_mixed, log_total = attend(query_rows, key_rows, value_rows)
    partial_value = jnp.dot(
        attn_mixed.reshape(row_count, local_width), attn_weight, preferred_element_type=F32
    )
    hidden_res = inputs + (links.sum_rows(partial_value, "tensor", active) + attn_bias)
    normed_out_b, normed_second, inv_second = layer_norm(hidden_res, norm_scale[1], norm_shift[1])
    outgoing = lax.dot_general(
        picks[0] + picks[1],
        normed_out_b.astype(BF16),
        (((0,), (0,)), ((), ())),
        preferred_element_type=F32,
    ).astype(BF16)
    received = links.exchange(
        outgoing.reshape(experts, capacity, model_width), ("expert",), active
    ).reshape(slots, model_width)
    pre_act = jnp.dot(received, expert_in, preferred_element_type=F32) + expert_in_bias
    activated = gelu_value(pre_act).astype(BF16)
    parts, part_shape = column_parts(activated, expert_out, experts, False)
    width = part_shape[2]
    own_bias = jnp.where(lax.axis_index("tensor") == 0, expert_out_bias, 0.0)
    parts = jnp.stack(
        [
            (part + own_bias[k * width : (k + 1) * width]).astype(BF16)
            for k, part in enumerate(parts)
        ]
    ).reshape(part_shape)
    landed = links.exchange(parts, ("tensor", "expert"), active)
    summed = jnp.sum(landed.reshape(members, slots, width).astype(F32), axis=0).astype(BF16)
    picked = jnp.einsum("jrn,nc->jrc", picks, summed, preferred_element_type=F32)
    branch = gate_rows[:, 0:1] * picked[0] + gate_rows[:, 1:2] * picked[1]
    block_out = hidden_res + links.join_columns(branch, active)
    kept_state = (
        normed_first,
        inv_first,
        normed_a,
        query_rows,
        key_rows,
        value_rows,
        attn_mixed,
        log_total,
        normed_second,
        inv_second,
        received,
        pre_act,
    )
    return (block_out, kept_state)


def backward_block(links, active, cotangent, weights, kept_state, picks, gate_rows):
    (
        norm_scale,
        norm_shift,
        proj_weight,
        proj_bias,
        attn_weight,
        attn_bias,
        expert_in,
        expert_in_bias,
        expert_out,
        expert_out_bias,
    ) = weights
    (
        normed_first,
        inv_first,
        normed_a,
        query_rows,
        key_rows,
        value_rows,
        attn_mixed,
        log_total,
        normed_second,
        inv_second,
        received,
        pre_act,
    ) = kept_state
    row_count, model_width = cotangent.shape
    experts = lax.axis_size("expert")
    members = lax.axis_size("tensor")
    slots = picks.shape[2]
    capacity = slots // experts
    local_width = proj_weight.shape[2]
    grad_rows = jnp.stack([(gate_rows[:, j : j + 1] * cotangent).astype(BF16) for j in range(TOPK)])
    outgoing = jnp.einsum("jrn,jrd->nd", picks, grad_rows, preferred_element_type=F32).astype(BF16)
    grad_out = links.exchange(
        outgoing.reshape(experts, capacity, model_width), ("expert",), active
    ).reshape(slots, model_width)
    grad_pre = lax.dot_general(
        grad_out, expert_out, (((1,), (1,)), ((), ())), preferred_element_type=F32
    ) * gelu_slope(pre_act)
    grad_expert_in_bias = jnp.sum(grad_pre, axis=0)
    grad_pre_b = grad_pre.astype(BF16)
    parts, part_shape = column_parts(grad_pre_b, expert_in, experts, True)
    parts = jnp.stack([part.astype(BF16) for part in parts]).reshape(part_shape)
    landed = links.exchange(parts, ("tensor", "expert"), active)
    summed = jnp.sum(landed.reshape(members, slots, part_shape[2]).astype(F32), axis=0).astype(BF16)
    grad_cols = jnp.dot(picks[0] + picks[1], summed, preferred_element_type=F32)
    grad_normed_b = links.join_columns(grad_cols, active)
    grad_hidden = cotangent + norm_back(grad_normed_b, normed_second, inv_second, norm_scale[1])
    grad_hidden_b = grad_hidden.astype(BF16)
    grad_mixed = (
        lax.dot_general(
            grad_hidden_b, attn_weight, (((1,), (1,)), ((), ())), preferred_element_type=F32
        )
        .astype(BF16)
        .reshape(attn_mixed.shape)
    )
    grad_query, grad_keys, grad_values = attend_back(
        query_rows, key_rows, value_rows, attn_mixed, log_total, grad_mixed
    )
    flats = [g.reshape(row_count, local_width) for g in (grad_query, grad_keys, grad_values)]
    grad_proj_bias = jnp.stack([jnp.sum(flats[0], axis=0), jnp.sum(flats[2], axis=0)])
    grad_proj = [flat.astype(BF16) for flat in flats]
    partial_norm = sum(
        lax.dot_general(
            grad_proj[k], proj_weight[:, k], (((1,), (1,)), ((), ())), preferred_element_type=F32
        )
        for k in range(3)
    )
    grad_normed_a = links.sum_rows(partial_norm, "tensor", active)
    grad_input = grad_hidden + norm_back(grad_normed_a, normed_first, inv_first, norm_scale[0])
    found = (
        grad_out,
        grad_pre_b,
        grad_expert_in_bias,
        grad_normed_b.astype(BF16),
        grad_hidden,
        grad_proj,
        grad_proj_bias,
        grad_normed_a.astype(BF16),
    )
    return (grad_input, found)


def weight_grads(links, kept_state, found):
    normed_first, _, normed_a, _, _, _, attn_mixed, _, normed_second, _, received, pre_act = (
        kept_state
    )
    (
        grad_out,
        grad_pre_b,
        grad_expert_in_bias,
        grad_normed_b,
        grad_hidden,
        grad_proj,
        grad_proj_bias,
        grad_normed_a,
    ) = found
    row_count, model_width = grad_hidden.shape
    experts = lax.axis_size("expert")

    def outer(left, right):
        return lax.dot_general(
            left, right, (((0,), (0,)), ((), ())), preferred_element_type=F32
        )

    grad_attn_bias = jnp.sum(grad_hidden, axis=0)
    grad_attn_weight = outer(attn_mixed.reshape(row_count, -1), grad_hidden.astype(BF16))
    grad_proj_weight = outer(normed_a, jnp.concatenate(grad_proj, axis=1))
    grad_normed_a, grad_normed_b = grad_normed_a.astype(F32), grad_normed_b.astype(F32)
    small = jnp.concatenate(
        [
            jnp.sum(grad_normed_a * normed_first, axis=0),
            jnp.sum(grad_normed_b * normed_second, axis=0),
            jnp.sum(grad_normed_a, axis=0),
            jnp.sum(grad_normed_b, axis=0),
            grad_attn_bias,
            grad_proj_bias.reshape(-1),
        ]
    )
    per_member = -(-small.size // (experts * 128)) * 128
    packed = jnp.pad(small, (0, experts * per_member - small.size)).reshape(experts, 1, per_member)
    proj_sum, attn_sum, small_sum = links.all_sum(
        [
            grad_proj_weight.astype(BF16).reshape(experts, -1, grad_proj_weight.shape[1]),
            grad_attn_weight.astype(BF16).reshape(experts, -1, model_width),
            packed,
        ],
        ("expert",),
        None,
    )
    activated = gelu_value(pre_act).astype(BF16)
    grad_expert_out = outer(activated, grad_out)
    grad_expert_out_bias = jnp.sum(grad_out, axis=0, dtype=F32)
    grad_expert_in = outer(received, grad_pre_b)
    small_sum = small_sum.reshape(-1)
    wide = small_sum[: 5 * model_width].reshape(5, model_width)
    return (
        wide[0:2],
        wide[2:4],
        proj_sum.astype(F32).reshape(model_width, 3, -1),
        small_sum[5 * model_width : small.size].reshape(grad_proj_bias.shape),
        attn_sum.astype(F32).reshape(grad_attn_weight.shape),
        wide[4],
        grad_expert_in[None],
        grad_expert_in_bias[None],
        grad_expert_out[None],
        grad_expert_out_bias[None],
    )


def on_device(
    inputs,
    cotangent,
    norm_scale,
    norm_shift,
    proj_weight,
    proj_bias,
    attn_weight,
    attn_bias,
    expert_in,
    expert_in_bias,
    expert_out,
    expert_out_bias,
    routes,
    gate_weights,
):
    weights = (
        norm_scale[0],
        norm_shift[0],
        proj_weight[0],
        proj_bias[0],
        attn_weight[0],
        attn_bias[0],
        expert_in[0, 0],
        expert_in_bias[0, 0],
        expert_out[0, 0],
        expert_out_bias[0, 0],
    )
    links = Links()
    is_first = lax.axis_index("section") == 0
    experts = lax.axis_size("expert")
    route_rows, gate_rows = routes[0, 0], gate_weights[0, 0]
    row_count = route_rows.shape[0]
    capacity = slot_count(row_count, experts)
    slot_ids = slot_table(route_rows, experts, capacity).reshape(row_count, TOPK)
    picks = (
        slot_ids.T[:, :, None] == jnp.arange(experts * capacity, dtype=jnp.int32)
    ).astype(BF16)

    def by_section(if_first, if_second):
        return jax.tree.map(
            lambda early, late: jnp.where(is_first, early, late), if_first, if_second
        )

    first_out, first_kept = forward_block(links, 0, inputs[0], weights, picks, gate_rows)
    passed_on = from_behind(first_out, "section", 1)
    second_out, second_kept = forward_block(links, 1, passed_on, weights, picks, gate_rows)
    kept_state = by_section(first_kept, second_kept)
    second_grad, second_found = backward_block(
        links, 1, cotangent[0], weights, kept_state, picks, gate_rows
    )
    sent_back = from_behind(second_grad, "section", -1)
    first_grad, first_found = backward_block(
        links, 0, sent_back, weights, kept_state, picks, gate_rows
    )
    found = by_section(first_found, second_found)
    section_out = by_section(first_out, second_out)
    section_in_grad = by_section(first_grad, second_grad)
    grads = weight_grads(links, kept_state, found)
    return (section_out[None, None], section_in_grad[None, None]) + tuple(g[None] for g in grads)


def solution(mesh):
    in_specs = (
        P(None, "expert", None),
        P(None, "expert", None),
        P("section", None, None),
        P("section", None, None),
        P("section", None, None, "tensor"),
        P("section", None, "tensor"),
        P("section", "tensor", None),
        P("section", None),
        P("section", "expert", None, "tensor"),
        P("section", "expert", "tensor"),
        P("section", "expert", "tensor", None),
        P("section", "expert", None),
        P("section", None, "expert", None),
        P("section", None, "expert", None),
    )
    out_specs = (
        P("section", None, "expert", None),
        P("section", None, "expert", None),
        P("section", None, None),
        P("section", None, None),
        P("section", None, None, "tensor"),
        P("section", None, "tensor"),
        P("section", "tensor", None),
        P("section", None),
        P("section", "expert", None, "tensor"),
        P("section", "expert", "tensor"),
        P("section", "expert", "tensor", None),
        P("section", "expert", None),
    )
    return jax.shard_map(
        on_device, mesh=mesh, in_specs=in_specs, out_specs=out_specs, check_vma=False
    )
```

time: 794 us -> 437 us (0.55)
  waiting for transfers between devices: 370 us -> 76.3 us
  Pallas kernels: 0 us -> 177 us
  blocking collectives: 132 us -> 0 us
  local copies, waits for them, and re-layouts: 126 us -> 73.9 us
  starting transfers between devices: 32.6 us -> 2.61 us
  between operations: 16.1 us -> 2.76 us
    psum x5 -> x0, waiting for transfers between devices: 195 us -> none  [the longest x2 81 us: forward_block(): hidden_res = inputs + (lax.psum(partial_value, 'tensor') + attn_bias)]
    pallas_call x0 -> x17, Pallas kernels: none -> 177 us  [call(): pl.pallas_call(kernel, out_shape=out_shape, in_specs=[in_vmem] * len(oper...]
    unnamed x13 -> x0, waiting for transfers between devices: 136 us -> none
    all_gather x4 -> x0, blocking collectives: 96.4 us -> none  [the longest x2 58.7 us: forward_block(): full_rows = lax.all_gather(produced, 'tensor', axis=2, tiled=True)]
    ppermute x2, waiting for transfers between devices: 4.23 us -> 76.3 us  [from_behind(): return lax.ppermute(block, axis, route)]
    unnamed x253 -> x237, local copies, waits for them, and re-layouts: 61.4 us -> 7.88 us
    all_to_all x7 -> x0, waiting for transfers between devices: 35.2 us -> none  [the longest x2 15 us: forward_block(): lax.all_to_all(outgoing, 'expert', split_axis=0, concat_axis=0, tiled=True)]
    all_to_all x7 -> x0, starting transfers between devices: 28.9 us -> none  [the longest x2 9.02 us: forward_block(): lax.all_to_all(outgoing, 'expert', split_axis=0, concat_axis=0, tiled=True)]
  transfers between devices with their start and end apart: 18 -> 2, of which waited for: 16 -> 1; matrix products, arithmetic and copies ran while one was open for 10% -> 3% of each run, Pallas kernels for 0% -> 1%
where the time goes in v1:
time: 437 us; the launch traced here: 433 us
  Pallas kernels  177 us (41%)
  waiting for transfers between devices  76.3 us (17%)
  local copies, waits for them, and re-layouts  73.9 us (17%)
  matrix products  56 us (13%)
  other arithmetic  43.9 us (10%)
    pallas_call x17, Pallas kernels, call(): pl.pallas_call(kernel, out_shape=out_shape, in_specs=[in_vmem] * len(oper...  177 us
    ppermute x2, waiting for transfers between devices, from_behind(): return lax.ppermute(block, axis, route)  76.3 us
    dot_general x4, matrix products, outer(): lax.dot_general(left, right, (((0,), (0,)), ((), ())), preferred_element_...  9.11 us
  transfers between devices with their start and end apart: 2, of which 1 were waited for; matrix products, arithmetic and copies ran while one was open for 3% of the time, Pallas kernels for 1%

profile of v1, /device:TPU:0, one launch (start us, length us, event | category | flops | bytes accessed | tf_op | source)
XLA Modules:
  0.0 432.6 jit_solution(18028525216620621233)
XLA Ops:
  0.7 2.2 reduce_sum.329
  15.6 17.7 %all_sum.5 = bf16[4,64,768]{2,1,0:T(8,128)(2,1)} custom-call(bf16[4,64,768]{2,1,0:T(8,128)(2,1)} %bitcast.417), custom_call_target="tpu_custom_call" | custom-call | tf_op jit(solution)/shard_map/all_sum/pallas_call | solution.py:151
  37.5 11.8 %exchange.8 = bf16[4,148,768]{2,1,0:T(8,128)(2,1)} custom-call(bf16[4,148,768]{2,1,0:T(8,128)(2,1)} %reshape.609.x_ref), custom_call_target="tpu_custom_call" | custom-call | tf_op jit(solution)/shard_map/exchange/pallas_call | solution.py:151
  49.3 2.3 reshape.610
  51.6 3.9 fusion.4
  59.0 2.3 copy.119
  61.3 2.2 reshape.611.x_ref
  63.5 20.1 %exchange.9 = bf16[16,148,192]{2,1,0:T(8,128)(2,1)} custom-call(bf16[16,148,192]{2,1,0:T(8,128)(2,1)} %reshape.611.x_ref), custom_call_target="tpu_custom_call" | custom-call | tf_op jit(solution)/shard_map/exchange/pallas_call | solution.py:151
  83.7 2.4 reshape.612
  86.1 1.6 reduce_sum.336
  88.8 12.8 %gather.4 = bf16[4,197,192]{2,1,0:T(8,128)(2,1)} custom-call(bf16[197,192]{1,0:T(8,128)(2,1)} %fusion.153.x_ref), custom_call_target="tpu_custom_call" | custom-call | tf_op jit(solution)/shard_map/gather/pallas_call | solution.py:151
  105.5 1.7 bitcast_convert_fusion.1
  107.2 2.3 reshape.623.x_ref
  109.5 2.4 exchange.12
  111.9 2.3 reshape.624
  115.5 1.3 fusion.56
  120.3 1.8 all_sum.6
  123.6 2.4 convolution_convert_fusion
  126.0 2.3 reshape.619.x_ref
  128.3 2.2 exchange.10
  130.5 2.3 reshape.620
  132.8 2.7 fusion.9
  138.5 2.4 fusion.178
  146.8 1.5 copy.124
  149.5 2.7 exchange.11
  152.2 1.6 reshape.622
  154.8 1.4 fusion.57
  157.0 1.7 gather.5
  158.8 1.8 slice_bitcast_fusion.30
  160.6 2.1 pad_maximum_fusion.2
  162.7 1.5 copy.130
  165.4 15.2 %exchange.13 = bf16[16,148,192]{2,1,0:T(8,128)(2,1)} custom-call(bf16[16,148,192]{2,1,0:T(8,128)(2,1)} %reshape.625.x_ref), custom_call_target="tpu_custom_call" | custom-call | tf_op jit(solution)/shard_map/exchange/pallas_call | solution.py:151
  180.6 2.4 reshape.626
  183.0 1.7 reduce_sum.343
  185.8 1.7 gather.6
  188.7 2.8 fusion.80
  196.6 1.8 all_sum.7
  198.5 1.4 fusion.79
  203.0 2.5 copy.145
  206.8 76.3 %collective-permute-done.1 = f32[197,768]{1,0:T(8,128)S(1)} collective-permute-done((f32[197,768]{1,0:T(8,128)}, f32[197,768]{1,0:T(8,128)S(1)}, u32[]{:S(2)}, u32[]{:S(2)}) %collective-permute-start.1) | collective-permute-done | bytes 605216 | tf_op jit(solution)/shard_map/ppermute | solution.py:30
  283.3 1.8 bitcast_convert_fusion
  285.1 2.3 reshape.631.x_ref
  287.4 11.7 %exchange.14 = bf16[4,148,768]{2,1,0:T(8,128)(2,1)} custom-call(bf16[4,148,768]{2,1,0:T(8,128)(2,1)} %reshape.631.x_ref), custom_call_target="tpu_custom_call" | custom-call | tf_op jit(solution)/shard_map/exchange/pallas_call | solution.py:151
  299.2 2.1 convert_reduce_fusion
  301.2 2.3 reshape.632
  303.5 5.2 %fusion.179 = (f32[768]{0:T(1024)}, bf16[592,768]{1,0:T(8,128)(2,1)S(1)}) fusion(f32[592,768]{1,0:T(8,128)} %copy-done.112, f32[592,768]{1,0:T(8,128)} %get-tuple-element.142, f32[768]{0:T(1024)S(1)} %copy-done.102, pred[]{:T(512)S(6)} %eq.42, bf16[592,768]{1,0:T(8,128)(2,1)} %reshape.632, bf16[1,1,768,768]{3,2,1,0:T(8,128)(2,1)} %param.24), kind=kOutput, calls=%fused_computation.364 | convolution fusion | flops 708807936 | bytes 6641665 | tf_op jit(solution)/shard_map/dot_general | solution.py:423
  308.8 3.0 convolution_bitcast_fusion
  311.8 2.7 convolution_bitcast_fusion.1
  317.5 2.4 copy.137
  319.9 2.2 reshape.633.x_ref
  322.1 20.2 %exchange.15 = bf16[16,148,192]{2,1,0:T(8,128)(2,1)} custom-call(bf16[16,148,192]{2,1,0:T(8,128)(2,1)} %reshape.633.x_ref), custom_call_target="tpu_custom_call" | custom-call | tf_op jit(solution)/shard_map/exchange/pallas_call | solution.py:151
  342.3 2.4 reshape.634
  344.8 2.4 reduce_sum.348
  347.1 1.9 convolution_convert_fusion.16
  349.1 1.6 copy.138.x_ref
  350.7 12.8 %gather.7 = bf16[4,197,192]{2,1,0:T(8,128)(2,1)} custom-call(bf16[197,192]{1,0:T(8,128)(2,1)} %copy.138.x_ref), custom_call_target="tpu_custom_call" | custom-call | tf_op jit(solution)/shard_map/gather/pallas_call | solution.py:151
  371.6 2.5 convolution_convert_fusion.2
  374.1 2.3 copy.143
  378.1 17.0 %all_sum.8 = bf16[4,64,768]{2,1,0:T(8,128)(2,1)} custom-call(bf16[4,64,768]{2,1,0:T(8,128)(2,1)} %bitcast.416), custom_call_target="tpu_custom_call" | custom-call | tf_op jit(solution)/shard_map/all_sum/pallas_call | solution.py:151
  395.1 1.4 fusion.69
  397.2 23.4 %all_sum.9 = (bf16[4,192,576]{2,1,0:T(8,128)(2,1)}, bf16[4,48,768]{2,1,0:T(8,128)(2,1)}, f32[4,1,1152]{2,1,0:T(1,128)}) custom-call(bf16[4,192,576]{2,1,0:T(8,128)(2,1)} %bitcast.401, bf16[4,48,768]{2,1,0:T(8,128)(2,1)} %bitcast.427, f32[4,1,1152]{2,1,0:T(1,128)} %reshape.641.refs_2_), custom_call_target="tpu_custom_call" | custom-call | tf_op jit(solution)/shard_map/all_sum/pallas_call | solution.py:151
  423.0 1.4 copy.146
  427.1 2.5 copy.144
  429.6 2.8 reshape.644
  (387 shorter events, 73.9 us)
Async XLA Ops:
  0.6 13.9 %copy-start = (bf16[1,192,768]{2,1,0:T(8,128)(2,1)S(1)}, bf16[1,192,768]{2,1,0:T(8,128)(2,1)}, u32[]{:S(2)}) copy-start(bf16[1,192,768]{2,1,0:T(8,128)(2,1)} %param.20) | copy-start | bytes 884740
  0.7 10.6 %copy-start.1 = (f32[1,197,768]{2,0,1:T(1,128)S(1)}, f32[1,197,768]{2,0,1:T(1,128)}, u32[]{:S(2)}) copy-start(f32[1,197,768]{2,0,1:T(1,128)} %param.14) | copy-start | bytes 1815556
  0.7 10.5 %copy-start.93 = (f32[1,2,768]{2,1,0:T(2,128)S(1)}, f32[1,2,768]{2,1,0:T(2,128)}, u32[]{:S(2)}) copy-start(f32[1,2,768]{2,1,0:T(2,128)} %param.17) | copy-start | bytes 18436
  0.7 10.5 %copy-start.94 = (f32[1,2,768]{2,1,0:T(2,128)S(1)}, f32[1,2,768]{2,1,0:T(2,128)}, u32[]{:S(2)}) copy-start(f32[1,2,768]{2,1,0:T(2,128)} %param.16) | copy-start | bytes 18436
  2.9 195.6 %copy-start.65 = (f32[197]{0:T(256)}, f32[197]{0:T(256)S(1)}, u32[]{:S(2)}) copy-start(f32[197]{0:T(256)S(1)} %broadcast_multiply_fusion.11) | copy-start | bytes 2368
  4.2 8.5 %copy-start.77 = (f32[197]{0:T(256)}, f32[197]{0:T(256)S(1)}, u32[]{:S(2)}) copy-start(f32[197]{0:T(256)S(1)} %multiply_reduce_fusion.7) | copy-start | bytes 2368
  4.2 8.2 %copy-start.12 = (bf16[1,768,3,192]{1,3,2,0:T(8,128)(2,1)S(1)}, bf16[1,768,3,192]{1,3,2,0:T(8,128)(2,1)}, u32[]{:S(2)}) copy-start(bf16[1,768,3,192]{1,3,2,0:T(8,128)(2,1)} %param.18) | copy-start | bytes 2654212
  4.2 194.2 %copy-start.73 = (f32[197]{0:T(256)}, f32[197]{0:T(256)S(1)}, u32[]{:S(2)}) copy-start(f32[197]{0:T(256)S(1)} %add_rsqrt_fusion.3) | copy-start | bytes 2368
  5.0 7.7 %copy-start.105 = (f32[1,1,192]{2,1,0:T(1,128)}, f32[1,1,192]{2,1,0:T(1,128)S(1)}, u32[]{:S(2)}) copy-start(f32[1,1,192]{2,1,0:T(1,128)S(1)} %get-tuple-element.133) | copy-start | bytes 2308
  5.0 8.0 %copy-start.103 = (f32[1,1,192]{2,1,0:T(1,128)}, f32[1,1,192]{2,1,0:T(1,128)S(1)}, u32[]{:S(2)}) copy-start(f32[1,1,192]{2,1,0:T(1,128)S(1)} %get-tuple-element.134) | copy-start | bytes 2308
  6.5 49.0 %copy-start.88 = (f32[1,1,192]{2,1,0:T(1,128)}, f32[1,1,192]{2,1,0:T(1,128)S(1)}, u32[]{:S(2)}) copy-start(f32[1,1,192]{2,1,0:T(1,128)S(1)} %get-tuple-element.128) | copy-start | bytes 2308
  6.5 49.6 %copy-start.86 = (f32[1,1,192]{2,1,0:T(1,128)}, f32[1,1,192]{2,1,0:T(1,128)S(1)}, u32[]{:S(2)}) copy-start(f32[1,1,192]{2,1,0:T(1,128)S(1)} %get-tuple-element.129) | copy-start | bytes 2308
  6.5 50.1 %copy-start.84 = (f32[1,1,192]{2,1,0:T(1,128)}, f32[1,1,192]{2,1,0:T(1,128)S(1)}, u32[]{:S(2)}) copy-start(f32[1,1,192]{2,1,0:T(1,128)S(1)} %get-tuple-element.130) | copy-start | bytes 2308
  6.5 50.8 %copy-start.82 = (f32[1,1,192]{2,1,0:T(1,128)}, f32[1,1,192]{2,1,0:T(1,128)S(1)}, u32[]{:S(2)}) copy-start(f32[1,1,192]{2,1,0:T(1,128)S(1)} %get-tuple-element.127) | copy-start | bytes 2308
  7.9 43.6 %copy-start.101 = (f32[768]{0:T(1024)}, f32[768]{0:T(1024)S(1)}, u32[]{:S(2)}) copy-start(f32[768]{0:T(1024)S(1)} %reduce.22) | copy-start | bytes 9220
  10.9 76.8 %copy-start.90 = (s32[2,197]{1,0:T(2,128)}, s32[2,197]{1,0:T(2,128)S(1)}, u32[]{:S(2)}) copy-start(s32[2,197]{1,0:T(2,128)S(1)} %copy.118) | copy-start | bytes 4732
  11.2 24.6 %copy-start.9 = (bf16[197,592]{1,0:T(8,128)(2,1)}, bf16[197,592]{1,0:T(8,128)(2,1)S(1)}, u32[]{:S(2)}) copy-start(bf16[197,592]{1,0:T(8,128)(2,1)S(1)} %fusion.146) | copy-start | bytes 699748
  11.2 104.1 %copy-start.62 = (f32[768]{0:T(1024)}, f32[768]{0:T(1024)S(1)}, u32[]{:S(2)}) copy-start(f32[768]{0:T(1024)S(1)} %get-tuple-element.79) | copy-start | bytes 9220
  11.2 188.6 %copy-start.59 = (f32[768]{0:T(1024)}, f32[768]{0:T(1024)S(1)}, u32[]{:S(2)}) copy-start(f32[768]{0:T(1024)S(1)} %get-tuple-element.156) | copy-start | bytes 9220
  51.6 3.9 copy-start.4
  101.6 3.8 copy-start.91
  102.9 4.3 copy-start.19
  102.9 11.3 %collective-permute-start = (f32[197,768]{1,0:T(8,128)S(1)}, f32[197,768]{1,0:T(8,128)S(1)}, u32[]{:S(2)}, u32[]{:S(2)}) collective-permute-start(f32[197,768]{1,0:T(8,128)S(1)} %convert_add_fusion), channel_id=1, source_target_pairs={{0,16},{1,17},{2,18},{3,19},{4,20},{5,21},{6,22},{7,23},{8,24},{9,... | collective-permute-start | bytes 1815560 | tf_op jit(solution)/shard_map/ppermute | solution.py:30
  115.3 3.4 copy-start.75
  115.3 84.6 %copy-start.71 = (f32[197]{0:T(256)}, f32[197]{0:T(256)S(1)}, u32[]{:S(2)}) copy-start(f32[197]{0:T(256)S(1)} %get-tuple-element.135) | copy-start | bytes 2368
  115.5 3.6 copy-start.54
  119.6 4.0 copy-start.81
  128.3 4.5 %copy-start.102 = (f32[768]{0:T(1024)S(1)}, f32[768]{0:T(1024)}, u32[]{:S(2)}) copy-start(f32[768]{0:T(1024)} %copy-done.101) | copy-start | bytes 9220
  132.8 3.4 copy-start.87
  140.9 3.5 copy-start.108
  154.8 5.8 %copy-start.56 = (bf16[1,592,192]{1,2,0:T(8,128)(2,1)S(1)}, bf16[1,592,192]{1,2,0:T(8,128)(2,1)}, u32[]{:S(2)}) copy-start(bf16[1,592,192]{1,2,0:T(8,128)(2,1)} %fusion.40) | copy-start | bytes 681988
  154.8 5.8 %copy-start.57 = (bf16[1,592,192]{1,2,0:T(8,128)(2,1)S(1)}, bf16[1,592,192]{1,2,0:T(8,128)(2,1)}, u32[]{:S(2)}) copy-start(bf16[1,592,192]{1,2,0:T(8,128)(2,1)} %fusion.39) | copy-start | bytes 681988
  154.8 5.8 %copy-start.58 = (bf16[1,592,192]{1,2,0:T(8,128)(2,1)S(1)}, bf16[1,592,192]{1,2,0:T(8,128)(2,1)}, u32[]{:S(2)}) copy-start(bf16[1,592,192]{1,2,0:T(8,128)(2,1)} %fusion.38) | copy-start | bytes 681988
  180.6 4.1 copy-start.10
  183.0 5.6 %copy-start.6 = (bf16[4,64,768]{2,1,0:T(8,128)(2,1)S(1)}, bf16[4,64,768]{2,1,0:T(8,128)(2,1)}, u32[]{:S(2)}) copy-start(bf16[4,64,768]{2,1,0:T(8,128)(2,1)} %all_sum.5) | copy-start | bytes 1179652
  183.0 5.6 %copy-start.79 = (f32[197]{0:T(256)S(1)}, f32[197]{0:T(256)}, u32[]{:S(2)}) copy-start(f32[197]{0:T(256)} %copy-done.78) | copy-start | bytes 2368
  183.0 5.6 %copy-start.96 = (f32[197]{0:T(256)S(1)}, f32[197]{0:T(256)}, u32[]{:S(2)}) copy-start(f32[197]{0:T(256)} %copy-done.95) | copy-start | bytes 2368
  195.2 3.2 copy-start.76
  201.7 81.4 %collective-permute-start.1 = (f32[197,768]{1,0:T(8,128)}, f32[197,768]{1,0:T(8,128)S(1)}, u32[]{:S(2)}, u32[]{:S(2)}) collective-permute-start(f32[197,768]{1,0:T(8,128)} %multiply_add_fusion.4), channel_id=1, source_target_pairs={{16,0},{17,1},{18,2},{19,3},{20,4},{21,5},{22,6},{23,7},{24,8},{25... | collective-permute-start | bytes 1815560 | tf_op jit(solution)/shard_map/ppermute | solution.py:30
  303.5 5.2 %copy-start.33 = (bf16[592,768]{1,0:T(8,128)(2,1)S(1)}, bf16[592,768]{1,0:T(8,128)(2,1)}, u32[]{:S(2)}) copy-start(bf16[592,768]{1,0:T(8,128)(2,1)} %reshape.624) | copy-start | bytes 2727940
  303.5 5.2 %copy-start.35 = (bf16[592,768]{1,0:T(8,128)(2,1)S(1)}, bf16[592,768]{1,0:T(8,128)(2,1)}, u32[]{:S(2)}) copy-start(bf16[592,768]{1,0:T(8,128)(2,1)} %reshape.632) | copy-start | bytes 2727940
  303.5 5.2 %copy-start.111 = (f32[592,768]{1,0:T(8,128)S(1)}, f32[592,768]{1,0:T(8,128)}, u32[]{:S(2)}) copy-start(f32[592,768]{1,0:T(8,128)} %get-tuple-element.142) | copy-start | bytes 5455876
  303.5 5.2 %copy-start.113 = (f32[592,768]{1,0:T(8,128)S(1)}, f32[592,768]{1,0:T(8,128)}, u32[]{:S(2)}) copy-start(f32[592,768]{1,0:T(8,128)} %copy-done.112) | copy-start | bytes 5455876
  342.3 4.8 %copy-start.11 = (bf16[197,592]{1,0:T(8,128)(2,1)S(1)}, bf16[197,592]{1,0:T(8,128)(2,1)}, u32[]{:S(2)}) copy-start(bf16[197,592]{1,0:T(8,128)(2,1)} %copy-done.9) | copy-start | bytes 699748
  344.7 19.9 %copy-start.22 = (bf16[197,192]{1,0:T(8,128)(2,1)S(1)}, bf16[197,192]{1,0:T(8,128)(2,1)}, u32[]{:S(2)}) copy-start(bf16[197,192]{1,0:T(8,128)(2,1)} %copy-done.21) | copy-start | bytes 226948
  344.7 19.9 %copy-start.24 = (bf16[197,192]{1,0:T(8,128)(2,1)S(1)}, bf16[197,192]{1,0:T(8,128)(2,1)}, u32[]{:S(2)}) copy-start(bf16[197,192]{1,0:T(8,128)(2,1)} %copy-done.23) | copy-start | bytes 226948
  344.8 19.9 %copy-start.26 = (bf16[197,192]{1,0:T(8,128)(2,1)S(1)}, bf16[197,192]{1,0:T(8,128)(2,1)}, u32[]{:S(2)}) copy-start(bf16[197,192]{1,0:T(8,128)(2,1)} %copy-done.25) | copy-start | bytes 226948
  368.4 3.3 copy-start.60
  368.4 3.2 copy-start.61
  368.4 3.2 copy-start.63
  368.4 3.2 copy-start.66
  371.6 4.8 %copy-start.15 = (bf16[1,768,3,192]{1,3,2,0:T(8,128)(2,1)S(1)}, bf16[1,768,3,192]{1,3,2,0:T(8,128)(2,1)}, u32[]{:S(2)}) copy-start(bf16[1,768,3,192]{1,3,2,0:T(8,128)(2,1)} %param.18) | copy-start | bytes 2654212
  376.7 18.4 %copy-start.3 = (f32[197,768]{1,0:T(8,128)S(1)}, f32[197,768]{1,0:T(8,128)}, u32[]{:S(2)}) copy-start(f32[197,768]{1,0:T(8,128)} %copy-done.2) | copy-start | bytes 1815556
  376.7 18.4 %copy-start.8 = (bf16[4,64,768]{2,1,0:T(8,128)(2,1)S(1)}, bf16[4,64,768]{2,1,0:T(8,128)(2,1)}, u32[]{:S(2)}) copy-start(bf16[4,64,768]{2,1,0:T(8,128)(2,1)} %all_sum.7) | copy-start | bytes 1179652
  377.0 19.5 %copy-start.64 = (f32[4224]{0:T(1024)S(1)}, f32[4224]{0:T(1024)}, u32[]{:S(2)}) copy-start(f32[4224]{0:T(1024)} %custom-call) | copy-start | bytes 50692
  377.0 19.5 %copy-start.69 = (f32[768]{0:T(1024)S(1)}, f32[768]{0:T(1024)}, u32[]{:S(2)}) copy-start(f32[768]{0:T(1024)} %get-tuple-element.66) | copy-start | bytes 9220
  377.0 19.5 %copy-start.68 = (f32[768]{0:T(1024)S(1)}, f32[768]{0:T(1024)}, u32[]{:S(2)}) copy-start(f32[768]{0:T(1024)} %get-tuple-element.97) | copy-start | bytes 9220
  377.0 19.5 %copy-start.70 = (f32[768]{0:T(1024)S(1)}, f32[768]{0:T(1024)}, u32[]{:S(2)}) copy-start(f32[768]{0:T(1024)} %get-tuple-element.81) | copy-start | bytes 9220
  378.1 43.5 %copy-start.67 = (f32[768]{0:T(1024)S(1)}, f32[768]{0:T(1024)}, u32[]{:S(2)}) copy-start(f32[768]{0:T(1024)} %convert_reduce_fusion) | copy-start | bytes 9220
  378.1 44.1 %copy-start.97 = (f32[768]{0:T(1024)S(1)}, f32[768]{0:T(1024)}, u32[]{:S(2)}) copy-start(f32[768]{0:T(1024)} %get-tuple-element.93) | copy-start | bytes 9220
  378.1 44.1 %copy-start.98 = (f32[768]{0:T(1024)S(1)}, f32[768]{0:T(1024)}, u32[]{:S(2)}) copy-start(f32[768]{0:T(1024)} %get-tuple-element.95) | copy-start | bytes 9220
  378.1 44.7 %copy-start.72 = (f32[197]{0:T(256)S(1)}, f32[197]{0:T(256)}, u32[]{:S(2)}) copy-start(f32[197]{0:T(256)} %copy-done.71) | copy-start | bytes 2368
  395.1 27.7 %copy-start.16 = (bf16[4,64,768]{2,1,0:T(8,128)(2,1)S(1)}, bf16[4,64,768]{2,1,0:T(8,128)(2,1)}, u32[]{:S(2)}) copy-start(bf16[4,64,768]{2,1,0:T(8,128)(2,1)} %all_sum.8) | copy-start | bytes 1179652
  422.7 3.5 copy-start.55
  (52 other events, 104.2 us)
